TPU v7x, 32 devices: a whole 2x2x4 slice. The times are simulated.
32 devices in a mesh: dp: 4 (over y, core), table: 8 (over z, x).
Axes of the slice: x: 2, y: 2, z: 4, core: 2. Of those that a mesh axis runs over, the one named last changes fastest.
Arguments:
- table: float32 [131072, 256], P(('dp', 'table')), may hold values from -6 to 6
- hidden: float32 [16384, 256], P(('dp', 'table')), may hold values from -24 to 24
- neg_ids: int32 [4, 8, 4, 128], P('dp', 'table'), may hold values from 0 to 4095
- pos_ids: int32 [16384], P(('dp', 'table')), may hold values from 0 to 4095
- dloss: float32 [16384], P(('dp', 'table')), may hold values from -4 to 4
Outputs:
- row_loss: float32 [16384], P(('dp', 'table'))
- grad_hidden: float32 [16384, 256], P(('dp', 'table'))
- grad_table: float32 [131072, 256], P(('dp', 'table'))
All inputs are finite; a program needn't handle non-finite values.
Results may differ from a plain program's by a relative error of at most 0.0003.
Values sent between devices are 32-bit elements; how exact they have to be, the bound alone decides.
A program may use at most 192 MiB of HBM per device.

v0:
```python
import math

import jax
import jax.numpy as jnp
from jax import lax
from jax.sharding import PartitionSpec as P


def local(table, hidden, neg_ids, pos_ids, dloss):
    feat_width = hidden.shape[1]
    logit_scale = 3.0 / math.sqrt(feat_width)
    dp_peers = lax.axis_size("dp")
    table_index = lax.axis_index("table")
    local_ids = neg_ids[0, 0]
    per_peer = local_ids.shape[1]
    local_count = dp_peers * per_peer
    own_rows = hidden.shape[0]
    outgoing = table[local_ids.reshape(-1)].reshape(dp_peers, per_peer, feat_width)
    candidates = lax.all_to_all(outgoing, "dp", split_axis=0, concat_axis=0, tiled=True).reshape(
        local_count, feat_width
    )
    row_side = jnp.stack([pos_ids.astype(jnp.float32), dloss], axis=1)
    group_hidden, group_side = (
        lax.all_gather(hidden, "table", axis=0, tiled=True),
        lax.all_gather(row_side, "table", axis=0, tiled=True),
    )
    targets = group_side[:, 0].astype(jnp.int32)
    weights = group_side[:, 1]
    logits = logit_scale * lax.dot_general(
        group_hidden,
        candidates,
        (((1,), (1,)), ((), ())),
        precision=lax.Precision.HIGHEST,
        preferred_element_type=jnp.float32,
    )
    offsets = table_index * local_count + lax.iota(jnp.int32, local_count)
    target_hits = offsets[None, :] == targets[:, None]
    logit_part = jnp.sum(jnp.where(target_hits, logits, 0.0), axis=1)
    local_max = jnp.max(logits, axis=1)
    row_max = lax.pmax(local_max, "table")
    exponent = jnp.exp(logits - row_max[:, None])
    row_total, target_logit = lax.psum((jnp.sum(exponent, axis=1), logit_part), "table")
    group_loss = row_max + jnp.log(row_total) - target_logit
    row_loss = lax.dynamic_slice_in_dim(group_loss, table_index * own_rows, own_rows, 0)
    coefficient = (
        logit_scale
        * weights[:, None]
        * (exponent / row_total[:, None] - target_hits.astype(jnp.float32))
    )
    grad_hidden = lax.psum_scatter(
        jnp.dot(
            coefficient,
            candidates,
            precision=lax.Precision.HIGHEST,
            preferred_element_type=jnp.float32,
        ),
        "table",
        scatter_dimension=0,
        tiled=True,
    )
    cand_grad = lax.dot_general(
        coefficient,
        group_hidden,
        (((0,), (0,)), ((), ())),
        precision=lax.Precision.HIGHEST,
        preferred_element_type=jnp.float32,
    )
    returned = lax.all_to_all(
        cand_grad.reshape(dp_peers, per_peer, feat_width),
        "dp",
        split_axis=0,
        concat_axis=0,
        tiled=True,
    )
    grad_table = (
        jnp.zeros(table.shape, jnp.float32)
        .at[local_ids.reshape(-1)]
        .add(returned.reshape(local_count, feat_width))
    )
    return (row_loss, grad_hidden, grad_table)


def solution(mesh):
    in_specs = (
        P(("dp", "table"), None),
        P(("dp", "table"), None),
        P("dp", "table", None, None),
        P(("dp", "table")),
        P(("dp", "table")),
    )
    out_specs = (P(("dp", "table")), P(("dp", "table"), None), P(("dp", "table"), None))
    return jax.shard_map(local, mesh=mesh, in_specs=in_specs, out_specs=out_specs, check_vma=False)
```

profile of v0, /device:TPU:0, one launch (start us, length us, event | category | flops | bytes accessed | tf_op | source)
XLA Modules:
  0.0 280.4 jit_solution(1260502819999587651)
XLA Ops:
  7.2 0.0 all-gather.2.cloned.1.call-start
  7.2 0.7 all-gather.2.cloned.1.call-update
  7.9 0.7 compare_select_fusion.1
  8.6 4.4 %gather_fusion = f32[512,256]{1,0:T(8,128)} fusion(f32[4096,256]{1,0:T(8,128)} %param.5, s32[1024]{0:T(1024)S(1)} %pad_clamp_fusion), kind=kCustom, calls=%fused_computation | custom fusion | bytes 1050624 | tf_op jit(solution)/shard_map/gather | solution.py:18
  13.0 4.3 %all-to-all-start = ((f32[4,128,256]{2,1,0:T(8,128)}), f32[4,128,256]{2,1,0:T(8,128)S(1)}, u32[]{:S(2)}, u32[]{:S(2)}) async-start(f32[4,128,256]{2,1,0:T(8,128)} %bitcast.2), calls=%async_computation | async-start | bytes 1048576 | tf_op jit(solution)/shard_map/all_to_all | solution.py:19
  17.3 0.0 reduce-scatter.2.cloned.1.call-start
  17.3 0.7 convert_element_type.10
  18.0 0.7 pad_maximum_fusion
  18.7 32.5 %all_gather.7 = f32[4096,2]{0,1:T(2,128)S(1)} all-gather(f32[512,2]{0,1:T(2,128)S(1)} %pad_maximum_fusion), channel_id=1, replica_groups=mesh['dp'=4,'table'=8] {'table'}, dimensions={0}, use_global_device_ids=true | all-gather | bytes 36864 | tf_op jit(solution)/shard_map/all_gather | solution.py:25
  51.2 0.0 all-to-all-done
  51.2 34.7 %all-gather.2.cloned.1.call-done = f32[4096,256]{1,0:T(8,128)} async-done(((f32[512,256]{1,0:T(8,128)}), f32[4096,256]{1,0:T(8,128)}) %all-gather.2.cloned.1.call-update) | async-done | bytes 4194320 | tf_op jit(solution)/shard_map/all_gather | solution.py:24
  85.9 10.9 %multiply_reduce_fusion = (f32[4096]{0:T(1024)S(1)}, f32[512,4096]{1,0:T(8,128)}) fusion(f32[512,256]{1,0:T(8,128)S(1)} %bitcast.25, f32[4096,256]{1,0:T(8,128)} %all-gather.2.cloned.1.call-done), kind=kOutput, calls=%fused_computation.10 | convolution fusion | flops 6446641152 | bytes 13123584 | tf_op jit(solution)/shard_map/dot_general | solution.py:29
  96.8 34.7 %pmax.7 = f32[4096]{0:T(1024)S(1)} all-reduce(f32[4096]{0:T(1024)S(1)} %get-tuple-element.9), channel_id=1, replica_groups=mesh['dp'=4,'table'=8] {'table'}, use_global_device_ids=true, to_apply=%region_1.2 | all-reduce | flops 4096 | bytes 32768 | tf_op jit(solution)/shard_map/pmax | solution.py:40
  131.5 4.7 %fusion.4 = (f32[4096]{0:T(1024)S(1)}, f32[4096]{0:T(1024)S(1)}) fusion(f32[512,4096]{1,0:T(8,128)} %get-tuple-element.10, f32[4096]{0:T(1024)S(1)} %pmax.7, s32[4096]{0:T(1024)S(1)} %bitcast.28, s32[512]{0:T(512)S(1)} %iota_add_fusion), kind=kLoop, calls=%fused_computation.9 | loop fusion | flops 12574720 | bytes 8456192 | tf_op jit(solution)/shard_map/reduce_sum | solution.py:42
  136.2 33.2 %all-reduce = (f32[4096]{0:T(1024)S(1)}, f32[4096]{0:T(1024)S(1)}) all-reduce(f32[4096]{0:T(1024)S(1)} %get-tuple-element.4, f32[4096]{0:T(1024)S(1)} %get-tuple-element.3), channel_id=1, replica_groups=mesh['dp'=4,'table'=8] {'table'}, use_global_device_ids=true, to_apply=%region_5.6 | all-reduce | flops 8192 | bytes 65536 | tf_op jit(solution)/shard_map/psum | solution.py:42
  169.4 18.5 %fusion.9 = f32[4096,256]{1,0:T(8,128)} fusion(f32[512,256]{1,0:T(8,128)S(1)} %bitcast.26, f32[512,4096]{1,0:T(8,128)} %get-tuple-element.10, f32[4096]{0:T(1024)S(1)} %get-tuple-element.6, f32[4096]{0:T(1024)S(1)} %bitcast.31, s32[4096]{0:T(1024)S(1)} %bitcast.29, f32[4096]{0:T(1024)S(1)} %pmax.7, s32[512]{0:T(512)S(1)} %iota_add_fusion), kind=kOutput, calls=%fused_computation.23 | convolution fusion | flops 6457131008 | bytes 13174784 | tf_op jit(solution)/shard_map/dot_general | solution.py:51
  187.9 0.0 reduce-scatter.2.cloned.1.call-update
  187.9 14.0 %fusion.7 = f32[512,256]{1,0:T(8,128)} fusion(f32[4096,256]{1,0:T(8,128)} %all-gather.2.cloned.1.call-done, f32[512,4096]{1,0:T(8,128)} %get-tuple-element.10, f32[4096]{0:T(1024)S(1)} %get-tuple-element.6, f32[4096]{0:T(1024)S(1)} %bitcast.32, s32[4096]{0:T(1024)S(1)} %bitcast.30, f32[4096]{0:T(1024)S(1)} %pmax.7, s32[512]{0:T(512)S(1)} %iota_add_fusion), kind=kOutput, calls=%fused_computation.22 | convolution fusion | flops 6457131008 | bytes 13174784 | tf_op jit(solution)/shard_map/dot_general | solution.py:61
  202.0 3.5 %all-to-all-start.1 = ((f32[4,128,256]{2,1,0:T(8,128)}), f32[4,128,256]{2,1,0:T(8,128)S(1)}, u32[]{:S(2)}, u32[]{:S(2)}) async-start(f32[4,128,256]{2,1,0:T(8,128)} %bitcast.9), calls=%async_computation.2 | async-start | bytes 1048576 | tf_op jit(solution)/shard_map/all_to_all | solution.py:68
  205.4 0.7 dynamic-slice_subtract_fusion
  206.1 8.1 %all-to-all-done.1 = f32[4,128,256]{2,1,0:T(8,128)S(1)} async-done(((f32[4,128,256]{2,1,0:T(8,128)}), f32[4,128,256]{2,1,0:T(8,128)S(1)}, u32[]{:S(2)}, u32[]{:S(2)}) %all-to-all-start.1) | async-done | bytes 524320 | tf_op jit(solution)/shard_map/all_to_all | solution.py:68
  214.2 5.5 %scatter_custom_fusion = f32[4096,256]{1,0:T(8,128)} fusion(s32[512]{0:T(512)S(1)} %bitcast.34, f32[512,256]{1,0:T(8,128)S(1)} %bitcast.27, f32[]{:T(128)} %constant.11.clone.1), kind=kCustom, calls=%fused_computation.11 | custom fusion | flops 131072 | bytes 4194308 | tf_op jit(solution)/shard_map/scatter-add | solution.py:78
  219.8 53.8 %reduce-scatter.2.cloned.1.call-done = f32[512,256]{1,0:T(8,128)} async-done(((f32[4096,256]{1,0:T(8,128)}), f32[512,256]{1,0:T(8,128)}) %reduce-scatter.2.cloned.1.call-update) | async-done | bytes 524304 | tf_op jit(solution)/shard_map/reduce_scatter | solution.py:50
  (3 shorter events, 0.0 us)
Async XLA Ops:
  7.2 78.7 %all-gather.2.cloned.1.call-start = ((), (), s32[]{:S(2)}) async-start(), calls=%async_computation.3 | async-start | bytes 4718592 | tf_op jit(solution)/shard_map/all_gather | solution.py:24
  13.0 38.2 %all-to-all-start = ((f32[4,128,256]{2,1,0:T(8,128)}), f32[4,128,256]{2,1,0:T(8,128)S(1)}, u32[]{:S(2)}, u32[]{:S(2)}) async-start(f32[4,128,256]{2,1,0:T(8,128)} %bitcast.2), calls=%async_computation | async-start | bytes 1048576 | tf_op jit(solution)/shard_map/all_to_all | solution.py:19
  17.3 256.3 %reduce-scatter.2.cloned.1.call-start = ((), (), s32[]{:S(2)}) async-start(), calls=%async_computation.4 | async-start | bytes 4718592 | tf_op jit(solution)/shard_map/reduce_scatter | solution.py:50
  202.0 12.3 %all-to-all-start.1 = ((f32[4,128,256]{2,1,0:T(8,128)}), f32[4,128,256]{2,1,0:T(8,128)S(1)}, u32[]{:S(2)}, u32[]{:S(2)}) async-start(f32[4,128,256]{2,1,0:T(8,128)} %bitcast.9), calls=%async_computation.2 | async-start | bytes 1048576 | tf_op jit(solution)/shard_map/all_to_all | solution.py:68
Sparse Core Ops, SparseCore 0:
  10.1 75.7 all-gather.1
  188.0 85.4 reduce-scatter.1
where the time goes:
time: 281 us; the launch traced here: 280 us
  blocking collectives  100 us (36%)
  waiting for transfers between devices  97.3 us (35%)
  matrix products  43.4 us (15%)
  between operations  14.1 us (5%)
  other arithmetic  13 us (5%)
  starting transfers between devices  7.78 us (3%)
  local copies, waits for them, and re-layouts  4.42 us (2%)
    reduce_scatter x1, waiting for transfers between devices, local(): lax.psum_scatter(jnp.dot(coefficient, candidates, precision=lax.Precision...  53.8 us
    pmax x1, blocking collectives, local(): row_max = lax.pmax(local_max, 'table')  34.7 us
    all_gather x1, waiting for transfers between devices, local(): lax.all_gather(hidden, 'table', axis=0, tiled=True)  34.7 us
    psum x1, blocking collectives, local(): lax.psum((jnp.sum(exponent, axis=1), logit_part), 'table')  33.2 us
    all_gather x1, blocking collectives, local(): lax.all_gather(row_side, 'table', axis=0, tiled=True)  32.5 us
    dot_general x1, matrix products, local(): jnp.dot(coefficient, candidates, precision=lax.Precision.HIGHEST, preferr...  18.5 us
    dot_general x1, matrix products, local(): lax.dot_general(coefficient, group_hidden, (((0,), (0,)), ((), ())), prec...  14 us
    dot_general x1, matrix products, local(): lax.dot_general(group_hidden, candidates, (((1,), (1,)), ((), ())), preci...  10.9 us
  transfers between devices with their start and end apart: 4, of which 3 were waited for; matrix products, arithmetic and copies ran while one was open for 10% of the time, Pallas kernels for 0%

commit v1 on v0

v1 whole, which is shorter than its diff:
```python
import math

import jax
import jax.numpy as jnp
from jax import lax
from jax.sharding import PartitionSpec as P


def local(table, hidden, neg_ids, pos_ids, dloss):
    feat_width = hidden.shape[1]
    logit_scale = 3.0 / math.sqrt(feat_width)
    dp_peers = lax.axis_size("dp")
    local_ids = neg_ids[0, 0]
    per_peer = local_ids.shape[1]
    local_count = dp_peers * per_peer
    outgoing = table[local_ids.reshape(-1)].reshape(dp_peers, per_peer, feat_width)
    own = lax.all_to_all(outgoing, "dp", split_axis=0, concat_axis=0, tiled=True).reshape(
        local_count, feat_width
    )
    candidates = lax.all_gather(own, "table", axis=0, tiled=True)
    pool = candidates.shape[0]
    high = dict(precision=lax.Precision.HIGH, preferred_element_type=jnp.float32)
    logits = logit_scale * lax.dot_general(hidden, candidates, (((1,), (1,)), ((), ())), **high)
    hits = lax.iota(jnp.int32, pool)[None, :] == pos_ids[:, None]
    target_logit = jnp.sum(jnp.where(hits, logits, 0.0), axis=1)
    row_max = jnp.max(logits, axis=1)
    exponent = jnp.exp(logits - row_max[:, None])
    row_total = jnp.sum(exponent, axis=1)
    row_loss = row_max + jnp.log(row_total) - target_logit
    coefficient = (
        logit_scale * dloss[:, None] * (exponent / row_total[:, None] - hits.astype(jnp.float32))
    )
    cand_grad = lax.dot_general(coefficient, hidden, (((0,), (0,)), ((), ())), **high)
    reduced = lax.psum_scatter(cand_grad, "table", scatter_dimension=0, tiled=True)
    grad_hidden = jnp.dot(coefficient, candidates, **high)
    returned = lax.all_to_all(
        reduced.reshape(dp_peers, per_peer, feat_width),
        "dp",
        split_axis=0,
        concat_axis=0,
        tiled=True,
    )
    grad_table = (
        jnp.zeros(table.shape, jnp.float32)
        .at[local_ids.reshape(-1)]
        .add(returned.reshape(local_count, feat_width))
    )
    return (row_loss, grad_hidden, grad_table)


def solution(mesh):
    in_specs = (
        P(("dp", "table"), None),
        P(("dp", "table"), None),
        P("dp", "table", None, None),
        P(("dp", "table")),
        P(("dp", "table")),
    )
    out_specs = (P(("dp", "table")), P(("dp", "table"), None), P(("dp", "table"), None))
    return jax.shard_map(local, mesh=mesh, in_specs=in_specs, out_specs=out_specs, check_vma=False)
```

time: 281 us -> 232 us (0.83)
  blocking collectives: 100 us -> 13 us
  waiting for transfers between devices: 97.3 us -> 160 us
  matrix products: 43.4 us -> 26.2 us
  starting transfers between devices: 7.78 us -> 3.73 us
  other arithmetic: 13 us -> 10.1 us
    all_gather x1, waiting for transfers between devices: 34.7 us -> 72.9 us  [local(): candidates = lax.all_gather(own, 'table', axis=0, tiled=True)]
    pmax x1 -> x0, blocking collectives: 34.7 us -> none  [local(): row_max = lax.pmax(local_max, 'table')]
    psum x1 -> x0, blocking collectives: 33.2 us -> none  [local(): lax.psum((jnp.sum(exponent, axis=1), logit_part), 'table')]
    reduce_scatter x1, waiting for transfers between devices: 53.8 us -> 87 us  [local(): lax.psum_scatter(cand_grad, 'table', scatter_dimension=0, tiled=True)]
    all_gather x1 -> x0, blocking collectives: 32.5 us -> none  [local(): lax.all_gather(row_side, 'table', axis=0, tiled=True)]
    dot_general x3, matrix products: 43.4 us -> 26.2 us  [the longest x1 13.4 us: local(): grad_hidden = jnp.dot(coefficient, candidates, **high)]
    all_to_all x0 -> x1, blocking collectives: none -> 13 us  [local(): lax.all_to_all(outgoing, 'dp', split_axis=0, concat_axis=0, tiled=True)]
    all_to_all x2 -> x1, waiting for transfers between devices: 8.11 us -> 0.01 us  [local(): lax.all_to_all(reduced.reshape(dp_peers, per_peer, feat_width), 'dp', spl...]
  transfers between devices with their start and end apart: 4 -> 3, of which waited for: 3 -> 2; matrix products, arithmetic and copies ran while one was open for 10% -> 6% of each run, Pallas kernels for 0% -> 0%
where the time goes in v1:
time: 232 us; the launch traced here: 231 us
  waiting for transfers between devices  160 us (69%)
  matrix products  26.2 us (11%)
  between operations  14.1 us (6%)
  blocking collectives  13 us (6%)
  other arithmetic  10.1 us (4%)
  local copies, waits for them, and re-layouts  4.47 us (2%)
  starting transfers between devices  3.73 us (2%)
    reduce_scatter x1, waiting for transfers between devices, local(): lax.psum_scatter(cand_grad, 'table', scatter_dimension=0, tiled=True)  87 us
    all_gather x1, waiting for transfers between devices, local(): candidates = lax.all_gather(own, 'table', axis=0, tiled=True)  72.9 us
    dot_general x1, matrix products, local(): grad_hidden = jnp.dot(coefficient, candidates, **high)  13.4 us
    all_to_all x1, blocking collectives, local(): lax.all_to_all(outgoing, 'dp', split_axis=0, concat_axis=0, tiled=True)  13 us
    dot_general x1, matrix products, local(): lax.dot_general(coefficient, hidden, (((0,), (0,)), ((), ())), **high)  7.17 us
    dot_general x1, matrix products, local(): lax.dot_general(hidden, candidates, (((1,), (1,)), ((), ())), **high)  5.59 us
    scatter-add x1, other arithmetic, local(): grad_table = jnp.zeros(table.shape, jnp.float32).at[local_ids.reshape(-1)...  5.54 us
  transfers between devices with their start and end apart: 3, of which 2 were waited for; matrix products, arithmetic and copies ran while one was open for 6% of the time, Pallas kernels for 0%

profile of v1, /device:TPU:0, one launch (start us, length us, event | category | flops | bytes accessed | tf_op | source)
XLA Modules:
  0.0 231.4 jit_solution(12281968755977844302)
XLA Ops:
  7.2 0.0 copy-start
  7.2 0.0 all-gather.2.cloned.1.call-start
  7.2 0.7 compare_select_fusion
  8.0 3.8 %gather_fusion = f32[512,256]{1,0:T(8,128)S(1)} fusion(f32[4096,256]{1,0:T(8,128)} %param.5, s32[1024]{0:T(1024)S(1)} %pad_clamp_fusion), kind=kCustom, calls=%fused_computation | custom fusion | bytes 1050624 | tf_op jit(solution)/shard_map/gather | solution.py:16
  11.7 13.0 %all_to_all.10 = f32[4,128,256]{2,1,0:T(8,128)} all-to-all(f32[4,128,256]{2,1,0:T(8,128)S(1)} %bitcast.23), channel_id=1, replica_groups=mesh['dp'=4,'table'=8] {'dp'}, dimensions={0} | all-to-all | bytes 1048576 | tf_op jit(solution)/shard_map/all_to_all | solution.py:17
  24.7 0.0 all-gather.2.cloned.1.call-update
  24.7 0.0 reduce-scatter.2.cloned.1.call-start
  24.8 0.7 broadcast_multiply_fusion
  25.5 0.0 copy-start.2
  25.5 72.9 %all-gather.2.cloned.1.call-done = f32[4096,256]{1,0:T(8,128)} async-done(((f32[512,256]{1,0:T(8,128)}), f32[4096,256]{1,0:T(8,128)}) %all-gather.2.cloned.1.call-update) | async-done | bytes 4194320 | tf_op jit(solution)/shard_map/all_gather | solution.py:20
  98.4 0.0 copy-done
  98.4 5.6 %multiply_reduce_fusion = (f32[512]{0:T(512)S(1)}, f32[4096,512]{1,0:T(8,128)S(1)}) fusion(f32[4096,256]{1,0:T(8,128)} %all-gather.2.cloned.1.call-done, f32[512,256]{1,0:T(8,128)S(1)} %copy-done), kind=kOutput, calls=%fused_computation.9 | convolution fusion | flops 3225419264 | bytes 13109248 | tf_op jit(solution)/shard_map/dot_general | solution.py:23
  104.0 0.0 copy-start.1
  104.0 0.0 copy-done.2
  104.0 2.5 %fusion.2 = (f32[512]{0:T(512)S(1)}, f32[512]{0:T(512)S(1)}) fusion(f32[4096,512]{1,0:T(8,128)S(1)} %get-tuple-element.6, f32[512]{0:T(512)S(1)} %get-tuple-element.5, s32[512]{0:T(512)S(1)} %copy-done.2), kind=kLoop, calls=%fused_computation.8 | loop fusion | flops 12581888 | bytes 8396800 | tf_op jit(solution)/shard_map/reduce_sum | solution.py:28
  106.5 0.7 copy-done.1
  107.2 7.2 %fusion.5 = f32[4096,256]{1,0:T(8,128)} fusion(f32[512,256]{1,0:T(8,128)S(1)} %copy-done, f32[4096,512]{1,0:T(8,128)S(1)} %get-tuple-element.6, f32[512]{0:T(512)S(1)} %get-tuple-element.3, f32[512]{0:T(512)S(1)} %broadcast_multiply_fusion, s32[512]{0:T(512)S(1)} %copy-done.2, f32[512]{0:T(512)S(1)} %get-tuple-element.5), kind=kOutput, calls=%fused_computation.12 | convolution fusion | flops 3235905536 | bytes 13115392 | tf_op jit(solution)/shard_map/dot_general | solution.py:33
  114.4 0.0 reduce-scatter.2.cloned.1.call-update
  114.4 87.0 %reduce-scatter.2.cloned.1.call-done = f32[512,256]{1,0:T(8,128)} async-done(((f32[4096,256]{1,0:T(8,128)}), f32[512,256]{1,0:T(8,128)}) %reduce-scatter.2.cloned.1.call-update) | async-done | bytes 524304 | tf_op jit(solution)/shard_map/reduce_scatter | solution.py:34
  201.4 3.6 %all-to-all-start.1 = ((f32[4,128,256]{2,1,0:T(8,128)}), f32[4,128,256]{2,1,0:T(8,128)S(1)}, u32[]{:S(2)}, u32[]{:S(2)}) async-start(f32[4,128,256]{2,1,0:T(8,128)} %bitcast.25), calls=%async_computation.2 | async-start | bytes 1048576 | tf_op jit(solution)/shard_map/all_to_all | solution.py:36
  205.1 13.4 %fusion.6 = f32[512,256]{1,0:T(8,128)} fusion(f32[4096,256]{1,0:T(8,128)} %all-gather.2.cloned.1.call-done, f32[4096,512]{1,0:T(8,128)} %copy-done.1, f32[512]{0:T(512)S(1)} %get-tuple-element.3, f32[512]{0:T(512)S(1)} %broadcast_multiply_fusion, s32[512]{0:T(512)S(1)} %copy-done.2, f32[512]{0:T(512)S(1)} %get-tuple-element.5), kind=kOutput, calls=%fused_computation.13 | convolution fusion | flops 3235905536 | bytes 13115392 | tf_op jit(solution)/shard_map/dot_general | solution.py:35
  218.5 0.6 add_subtract_fusion
  219.1 0.0 all-to-all-done.1
  219.1 5.5 %scatter_custom_fusion = f32[4096,256]{1,0:T(8,128)} fusion(s32[512]{0:T(512)S(1)} %bitcast.28, f32[512,256]{1,0:T(8,128)S(1)} %bitcast.26, f32[]{:T(128)} %constant.2.clone.1), kind=kCustom, calls=%fused_computation.10 | custom fusion | flops 131072 | bytes 4194308 | tf_op jit(solution)/shard_map/scatter-add | solution.py:46
  (1 shorter events, 0.0 us)
Async XLA Ops:
  7.2 91.2 %copy-start = (f32[512,256]{1,0:T(8,128)S(1)}, f32[512,256]{1,0:T(8,128)}, u32[]{:S(2)}) copy-start(f32[512,256]{1,0:T(8,128)} %param.6) | copy-start | bytes 1572868
  7.2 91.2 %all-gather.2.cloned.1.call-start = ((), (), s32[]{:S(2)}) async-start(), calls=%async_computation.3 | async-start | bytes 4718592 | tf_op jit(solution)/shard_map/all_gather | solution.py:20
  24.7 176.7 %reduce-scatter.2.cloned.1.call-start = ((), (), s32[]{:S(2)}) async-start(), calls=%async_computation.4 | async-start | bytes 4718592 | tf_op jit(solution)/shard_map/reduce_scatter | solution.py:34
  25.5 78.5 %copy-start.2 = (s32[512]{0:T(512)S(1)}, s32[512]{0:T(512)}, u32[]{:S(2)}) copy-start(s32[512]{0:T(512)} %param.8) | copy-start | bytes 6148
  104.0 3.2 %copy-start.1 = (f32[4096,512]{1,0:T(8,128)}, f32[4096,512]{1,0:T(8,128)S(1)}, u32[]{:S(2)}) copy-start(f32[4096,512]{1,0:T(8,128)S(1)} %get-tuple-element.6) | copy-start | bytes 25165828
  201.4 17.6 %all-to-all-start.1 = ((f32[4,128,256]{2,1,0:T(8,128)}), f32[4,128,256]{2,1,0:T(8,128)S(1)}, u32[]{:S(2)}, u32[]{:S(2)}) async-start(f32[4,128,256]{2,1,0:T(8,128)} %bitcast.25), calls=%async_computation.2 | async-start | bytes 1048576 | tf_op jit(solution)/shard_map/all_to_all | solution.py:36
Sparse Core Ops, SparseCore 0:
  24.9 73.4 all-gather.1
  114.5 86.8 reduce-scatter.1

commit v2 on v1

v2 whole, which is shorter than its diff:
```python
import functools
import math

import jax
import jax.numpy as jnp
from jax import lax
from jax.experimental import pallas as pl
from jax.experimental.pallas import tpu as pltpu
from jax.sharding import PartitionSpec as P

MESH = pl.DeviceIdType.MESH


def split(x):
    high = x.astype(jnp.bfloat16)
    return high, (x - high.astype(jnp.float32)).astype(jnp.bfloat16)


def kernel(
    peers, near, scale, piece,
    out_ref, hid_ref, side_ref,
    loss_ref, gh_ref, back_ref,
    cand, ct_hi, ct_lo, hid, h_hi, h_lo, side, expo, bstat, stat, cg, xrecv, ret, ght, ghrecv,
    local_sem, c_send, c_recv, r_send, r_recv, h_send, h_recv, d_send, d_recv,
    t_send, t_recv, x_send, x_recv, z_send, z_recv, g_send, g_recv,
):
    me = lax.axis_index("dp")
    t = lax.axis_index("table")
    hi, lo, s = t // (near * 2), lax.rem(t // 2, near), lax.rem(t, 2)
    rows, width = hid_ref.shape
    per = out_ref.shape[1]
    count = peers * per
    group = piece // per
    subs = peers // group

    def place(far, mid, last):
        return far * (near * 2) + mid * 2 + last

    def owner(dh, dg):
        return (lax.rem(me + dg, peers), place(lax.rem(hi + dh, 2), lo, s))

    def across(da):
        return (me, place(hi, lax.rem(lo + da, near), s))

    beside = (me, place(hi, lo, 1 - s))
    reach = [(dh, dg) for dh in (1, 0) for dg in range(peers) if (dh, dg) != (0, 0)]

    barrier = pltpu.get_barrier_semaphore()
    others = [owner(*r) for r in reach] + [across(da) for da in range(1, near)] + [beside]
    for other in others:
        pl.semaphore_signal(barrier, inc=1, device_id=other, device_id_type=MESH)
    pl.semaphore_wait(barrier, len(others))

    started = []

    def send(src, dst, ssem, rsem, dev):
        copy = pltpu.make_async_remote_copy(
            src_ref=src, dst_ref=dst, send_sem=ssem, recv_sem=rsem, device_id=dev, device_id_type=MESH
        )
        copy.start()
        started.append(copy)
        return copy

    own_copy = pltpu.make_async_copy(out_ref.at[me], cand.at[0, 0, me], local_sem)
    own_copy.start()
    first = {}
    for dh, dg in reach:
        first[dh, dg] = send(
            out_ref.at[lax.rem(me + dg, peers)], cand.at[dh, 0, me],
            c_send.at[dh, dg], c_recv.at[dh, dg], owner(dh, dg),
        )
    hids = []
    for da in range(1, near):
        hids.append(send(side_ref, side.at[lo], d_send.at[da], d_recv.at[da], across(da)))
        hids.append(send(hid_ref, hid.at[da - 1], h_send.at[da], h_recv.at[da], across(da)))

    side[lo] = side_ref[...]
    top, low = split(hid_ref[...])
    h_hi[lo] = top
    h_lo[lo] = low
    ght[...] = jnp.zeros_like(ght)

    relays = {}

    def relay(dh):
        for dg in range(peers):
            source = lax.rem(me + peers - dg, peers)
            if (dh, dg) == (0, 0):
                own_copy.wait()
            else:
                first[dh, dg].wait_recv()
            relays[dh, dg] = send(
                cand.at[dh, 0, source], cand.at[dh, 1, source],
                r_send.at[dh, dg], r_recv.at[dh, dg], beside,
            )

    def hits(dh, ds, j, mid):
        base = place(lax.rem(hi + dh, 2), lo, lax.rem(s + ds, 2)) * count + j * piece
        index = lax.broadcasted_iota(jnp.int32, (piece, rows), 0) + base
        return index == side[mid, 0:1, :].astype(jnp.int32)

    def forward(dh, ds):
        for j in range(subs):
            block = cand[dh, ds, j * group : (j + 1) * group].reshape(piece, width)
            b_hi, b_lo = split(block)
            turned = split(block.T)
            ct_hi[dh, ds, j] = turned[0]
            ct_lo[dh, ds, j] = turned[1]
            left = jnp.concatenate([b_hi, b_lo, b_hi], axis=1)

            def step(mid, carry):
                right = jnp.concatenate([h_hi[mid], h_hi[mid], h_lo[mid]], axis=1)
                logits = scale * lax.dot_general(
                    left, right, (((1,), (1,)), ((), ())), preferred_element_type=jnp.float32
                )
                peak = jnp.max(logits, axis=0, keepdims=True)
                power = jnp.exp(logits - peak)
                expo[dh, ds, j, mid] = power
                bstat[dh, ds, j, mid, 0:1, :] = peak
                bstat[dh, ds, j, mid, 1:2, :] = jnp.sum(power, axis=0, keepdims=True)
                bstat[dh, ds, j, mid, 2:3, :] = jnp.sum(
                    jnp.where(hits(dh, ds, j, mid), logits, 0.0), axis=0, keepdims=True
                )
                return carry

            lax.fori_loop(0, near, step, 0)

    def wait_relays(dh):
        for dg in range(peers):
            relays[dh, dg].wait_recv()

    relay(0)
    for copy in hids:
        copy.wait_recv()
    for da in range(1, near):
        mid = lax.rem(lo + near - da, near)
        top, low = split(hid[da - 1])
        h_hi[mid] = top
        h_lo[mid] = low
    forward(0, 0)
    wait_relays(0)
    relay(1)
    forward(0, 1)
    forward(1, 0)
    wait_relays(1)
    forward(1, 1)

    parts = [(dh, ds, j) for dh in (0, 1) for ds in (0, 1) for j in range(subs)]

    def gather_stats(mid, carry):
        peak = bstat[0, 0, 0, mid, 0:1, :]
        for p in parts[1:]:
            peak = jnp.maximum(peak, bstat[p[0], p[1], p[2], mid, 0:1, :])
        total = jnp.zeros_like(peak)
        target = jnp.zeros_like(peak)
        for p in parts:
            total += bstat[p[0], p[1], p[2], mid, 1:2, :] * jnp.exp(
                bstat[p[0], p[1], p[2], mid, 0:1, :] - peak
            )
            target += bstat[p[0], p[1], p[2], mid, 2:3, :]
        stat[lo, mid] = jnp.concatenate([peak, total, target] + [target] * 5, axis=0)
        return carry

    lax.fori_loop(0, near, gather_stats, 0)
    talks = [
        send(stat.at[lo], stat.at[lo], t_send.at[da], t_recv.at[da], across(da))
        for da in range(1, near)
    ]
    for copy in talks:
        copy.wait_recv()

    def merged(mid):
        peak = stat[0, mid, 0:1, :]
        for a in range(1, near):
            peak = jnp.maximum(peak, stat[a, mid, 0:1, :])
        total = jnp.zeros_like(peak)
        target = jnp.zeros_like(peak)
        for a in range(near):
            total += stat[a, mid, 1:2, :] * jnp.exp(stat[a, mid, 0:1, :] - peak)
            target += stat[a, mid, 2:3, :]
        return peak, total, target

    peak, total, target = merged(lo)
    loss_ref[...] = peak + jnp.log(total) - target

    def backward(dh, ds):
        for j in range(subs):
            flip = jnp.concatenate([ct_hi[dh, ds, j], ct_hi[dh, ds, j], ct_lo[dh, ds, j]], axis=1)

            def step(mid, acc):
                peak, total, _ = merged(mid)
                weight = scale * side[mid, 1:2, :]
                factor = weight * jnp.exp(bstat[dh, ds, j, mid, 0:1, :] - peak) / total
                power = expo[dh, ds, j, mid] * factor
                c_hi, c_lo = split(jnp.where(hits(dh, ds, j, mid), power - weight, power))
                ght[mid] += jnp.dot(
                    flip, jnp.concatenate([c_hi, c_lo, c_hi], axis=0),
                    preferred_element_type=jnp.float32,
                )
                return acc + jnp.dot(
                    jnp.concatenate([c_hi, c_lo, c_hi], axis=1),
                    jnp.concatenate([h_hi[mid], h_hi[mid], h_lo[mid]], axis=0),
                    preferred_element_type=jnp.float32,
                )

            acc = lax.fori_loop(0, near, step, jnp.zeros((piece, width), jnp.float32))
            cg[dh, ds, j * group : (j + 1) * group] = acc.reshape(group, per, width)

    sides = {}

    def send_side(dh):
        for dg in range(peers):
            source = lax.rem(me + dg, peers)
            sides[dh, dg] = send(
                cg.at[dh, 1, source], xrecv.at[dh, source],
                x_send.at[dh, dg], x_recv.at[dh, dg], beside,
            )

    finals = []

    def finish(dh, first_dg, last_dg):
        for dg in range(first_dg, last_dg):
            source = lax.rem(me + dg, peers)
            sides[dh, dg].wait_recv()
            value = cg[dh, 0, source] + xrecv[dh, source]
            if (dh, dg) == (0, 0):
                ret[0, me] = value
            else:
                cg[dh, 0, source] = value
                finals.append(
                    send(
                        cg.at[dh, 0, source], ret.at[dh, me],
                        z_send.at[dh, dg], z_recv.at[dh, dg], owner(dh, dg),
                    )
                )

    backward(1, 1)
    send_side(1)
    backward(1, 0)
    backward(0, 1)
    send_side(0)
    finish(1, 0, peers // 2)
    backward(0, 0)
    grads = [
        send(ght.at[lax.rem(lo + da, near)], ghrecv.at[da - 1], g_send.at[da], g_recv.at[da], across(da))
        for da in range(1, near)
    ]
    finish(1, peers // 2, peers)
    finish(0, 0, peers)
    for copy in grads:
        copy.wait_recv()
    whole = ght[lo]
    for da in range(1, near):
        whole += ghrecv[da - 1]
    gh_ref[...] = whole.T
    for copy in finals:
        copy.wait_recv()
    back_ref[...] = ret[0] + ret[1]
    for copy in started:
        copy.wait_send()


def local(table, hidden, neg_ids, pos_ids, dloss):
    rows, width = hidden.shape
    scale = 3.0 / math.sqrt(width)
    peers = lax.axis_size("dp")
    near = lax.axis_size("table") // 4
    flat_ids = neg_ids[0, 0].reshape(-1)
    per = neg_ids.shape[3]
    count = peers * per
    piece = math.gcd(512, count)
    subs = count // piece
    outgoing = table.at[flat_ids].get(mode="promise_in_bounds").reshape(peers, per, width)
    side = jnp.stack([pos_ids.astype(jnp.float32), dloss] + [dloss] * 6, axis=0)
    f32, bf16 = jnp.float32, jnp.bfloat16
    pairs = pltpu.SemaphoreType.DMA((2, peers))
    nears = pltpu.SemaphoreType.DMA((near,))
    vmem = pl.BlockSpec(memory_space=pltpu.VMEM)
    flops = 18 * 4 * count * near * rows * width
    loss, grad_hidden, returned = pl.pallas_call(
        functools.partial(kernel, peers, near, scale, piece),
        out_shape=(
            jax.ShapeDtypeStruct((1, rows), f32),
            jax.ShapeDtypeStruct((rows, width), f32),
            jax.ShapeDtypeStruct((peers, per, width), f32),
        ),
        in_specs=[vmem] * 3,
        out_specs=(vmem,) * 3,
        scratch_shapes=[
            pltpu.VMEM((2, 2, peers, per, width), f32),
            pltpu.VMEM((2, 2, subs, width, piece), bf16),
            pltpu.VMEM((2, 2, subs, width, piece), bf16),
            pltpu.VMEM((max(near - 1, 1), rows, width), f32),
            pltpu.VMEM((near, rows, width), bf16),
            pltpu.VMEM((near, rows, width), bf16),
            pltpu.VMEM((near, 8, rows), f32),
            pltpu.VMEM((2, 2, subs, near, piece, rows), f32),
            pltpu.VMEM((2, 2, subs, near, 8, rows), f32),
            pltpu.VMEM((near, near, 8, rows), f32),
            pltpu.VMEM((2, 2, peers, per, width), f32),
            pltpu.VMEM((2, peers, per, width), f32),
            pltpu.VMEM((2, peers, per, width), f32),
            pltpu.VMEM((near, width, rows), f32),
            pltpu.VMEM((max(near - 1, 1), width, rows), f32),
            pltpu.SemaphoreType.DMA,
            pairs, pairs, pairs, pairs, nears, nears, nears, nears,
            nears, nears, pairs, pairs, pairs, pairs, nears, nears,
        ],
        compiler_params=pltpu.CompilerParams(
            collective_id=0, has_side_effects=True, vmem_limit_bytes=67043328
        ),
        cost_estimate=pl.CostEstimate(flops=flops, bytes_accessed=4 * count * width, transcendentals=0),
    )(outgoing, hidden, side)
    grad_table = (
        jnp.zeros(table.shape, f32)
        .at[flat_ids]
        .add(returned.reshape(count, width), mode="promise_in_bounds")
    )
    return (loss.reshape(rows), grad_hidden, grad_table)


def solution(mesh):
    in_specs = (
        P(("dp", "table"), None),
        P(("dp", "table"), None),
        P("dp", "table", None, None),
        P(("dp", "table")),
        P(("dp", "table")),
    )
    out_specs = (P(("dp", "table")), P(("dp", "table"), None), P(("dp", "table"), None))
    return jax.shard_map(local, mesh=mesh, in_specs=in_specs, out_specs=out_specs, check_vma=False)
```

time: 232 us -> 98.6 us (0.42)
  waiting for transfers between devices: 160 us -> 0 us
  Pallas kernels: 0 us -> 81.4 us
  matrix products: 26.2 us -> 0 us
  between operations: 14.1 us -> 0.66 us
  blocking collectives: 13 us -> 0 us
  starting transfers between devices: 3.73 us -> 0 us
  local copies, waits for them, and re-layouts: 4.47 us -> 7.37 us
  other arithmetic: 10.1 us -> 7.58 us
    reduce_scatter x1 -> x0, waiting for transfers between devices: 87 us -> none  [local(): lax.psum_scatter(cand_grad, 'table', scatter_dimension=0, tiled=True)]
    pallas_call x0 -> x1, Pallas kernels: none -> 81.4 us  [local(): pl.pallas_call(functools.partial(kernel, peers, near, scale, piece), out_...]
    all_gather x1 -> x0, waiting for transfers between devices: 72.9 us -> none  [local(): candidates = lax.all_gather(own, 'table', axis=0, tiled=True)]
    dot_general x3 -> x0, matrix products: 26.2 us -> none  [the longest x1 13.4 us: local(): grad_hidden = jnp.dot(coefficient, candidates, **high)]
    all_to_all x1 -> x0, blocking collectives: 13 us -> none  [local(): lax.all_to_all(outgoing, 'dp', split_axis=0, concat_axis=0, tiled=True)]
    all_to_all x1 -> x0, starting transfers between devices: 3.65 us -> none  [local(): lax.all_to_all(reduced.reshape(dp_peers, per_peer, feat_width), 'dp', spl...]
    reduce_sum x1 -> x0, other arithmetic: 2.5 us -> none  [local(): row_total = jnp.sum(exponent, axis=1)]
  transfers between devices with their start and end apart: 3 -> 0, of which waited for: 2 -> 0; matrix products, arithmetic and copies ran while one was open for 6% -> 0% of each run, Pallas kernels for 0% -> 0%
where the time goes in v2:
time: 98.6 us; the launch traced here: 97 us
  Pallas kernels  81.4 us (83%)
  other arithmetic  7.58 us (8%)
  local copies, waits for them, and re-layouts  7.37 us (7%)
    pallas_call x1, Pallas kernels, local(): pl.pallas_call(functools.partial(kernel, peers, near, scale, piece), out_...  81.4 us
    scatter-add x1, other arithmetic, local(): grad_table = jnp.zeros(table.shape, f32).at[flat_ids].add(returned.reshap...  6.21 us
    gather x1, local copies, waits for them, and re-layouts, local(): table.at[flat_ids].get(mode='promise_in_bounds').reshape(peers, per, width)  4.41 us

profile of v2, /device:TPU:0, one launch (start us, length us, event | category | flops | bytes accessed | tf_op | source)
XLA Modules:
  0.0 97.0 jit_solution(3899289394767309571)
XLA Ops:
  0.6 0.7 compare_select_fusion
  1.3 0.0 copy-start.1
  1.3 0.7 convert_element_type.3
  2.0 0.0 copy-done.1
  2.0 1.6 %stack.8.side_ref = f32[8,512]{1,0:T(8,128)} concatenate(f32[1,512]{1,0:T(1,128)S(1)} %bitcast.17, f32[1,512]{1,0:T(1,128)} %bitcast.8, f32[1,512]{1,0:T(1,128)} %bitcast.9, f32[1,512]{1,0:T(1,128)} %bitcast.10, f32[1,512]{1,0:T(1,128)} %bitcast.11, f32[1,512]{1,0:T(1,128)} %bitcast.12, f32[1,512]{1,0:T(1,128)} %bitcast.13, f32[1,512]{1,0:T(1,128)} %bitcast.14), dimensions={0} | concatenate | bytes 32768 | tf_op jit(solution)/shard_map/stack | solution.py:274
  3.6 4.4 %gather_fusion = f32[512,256]{1,0:T(8,128)} fusion(f32[4096,256]{1,0:T(8,128)} %param.5, s32[1024]{0:T(1024)S(1)} %pad_clamp_fusion), kind=kCustom, calls=%fused_computation | custom fusion | bytes 1050624 | tf_op jit(solution)/shard_map/gather | solution.py:273
  8.0 81.4 %shard_map.76 = (f32[1,512]{1,0:T(1,128)}, f32[512,256]{1,0:T(8,128)}, f32[4,128,256]{2,1,0:T(8,128)}) custom-call(f32[4,128,256]{2,1,0:T(8,128)} %bitcast.7, f32[512,256]{1,0:T(8,128)} %hid_ref.1, f32[8,512]{1,0:T(8,128)} %stack.8.side_ref), custom_call_target="tpu_custom_call" | custom-call | flops 9663676416 | bytes 524288 | tf_op jit(solution)/shard_map/pallas_call | solution.py:280
  89.4 0.0 copy-start.2
  89.4 0.0 copy-start
  89.4 6.2 %scatter_custom_fusion = f32[4096,256]{1,0:T(8,128)} fusion(s32[512]{0:T(512)} %bitcast.16, f32[512,256]{1,0:T(8,128)} %bitcast.20, f32[]{:T(128)} %constant.2.clone.1), kind=kCustom, calls=%fused_computation.2 | custom fusion | flops 131072 | bytes 4194816 | tf_op jit(solution)/shard_map/scatter-add | solution.py:317
  95.6 0.0 copy-done.2
  95.6 0.6 copy.10
  96.2 0.0 copy-done
  96.2 0.8 copy.11
  (1 shorter events, 0.0 us)
Async XLA Ops:
  1.3 0.7 copy-start.1
  89.4 6.2 %copy-start.2 = (f32[1,512]{1,0:T(1,128)S(1)}, f32[1,512]{1,0:T(1,128)}, u32[]{:S(2)}) copy-start(f32[1,512]{1,0:T(1,128)} %get-tuple-element.6) | copy-start | bytes 6148
  89.4 6.8 %copy-start = (f32[512,256]{1,0:T(8,128)S(1)}, f32[512,256]{1,0:T(8,128)}, u32[]{:S(2)}) copy-start(f32[512,256]{1,0:T(8,128)} %get-tuple-element.13) | copy-start | bytes 1572868

commit v3 on v2

--- a/solution.py
+++ b/solution.py
@@ -43,7 +43,7 @@
         return (me, place(hi, lax.rem(lo + da, near), s))
 
     beside = (me, place(hi, lo, 1 - s))
-    reach = [(dh, dg) for dh in (1, 0) for dg in range(peers) if (dh, dg) != (0, 0)]
+    reach = [(dh, dg) for dh in (0, 1) for dg in range(peers) if (dh, dg) != (0, 0)]
 
     barrier = pltpu.get_barrier_semaphore()
     others = [owner(*r) for r in reach] + [across(da) for da in range(1, near)] + [beside]
@@ -64,15 +64,21 @@
     own_copy = pltpu.make_async_copy(out_ref.at[me], cand.at[0, 0, me], local_sem)
     own_copy.start()
     first = {}
-    for dh, dg in reach:
-        first[dh, dg] = send(
-            out_ref.at[lax.rem(me + dg, peers)], cand.at[dh, 0, me],
-            c_send.at[dh, dg], c_recv.at[dh, dg], owner(dh, dg),
-        )
     hids = []
+
+    def push(far):
+        for dh, dg in reach:
+            if dh == far:
+                first[dh, dg] = send(
+                    out_ref.at[lax.rem(me + dg, peers)], cand.at[dh, 0, me],
+                    c_send.at[dh, dg], c_recv.at[dh, dg], owner(dh, dg),
+                )
+
+    push(0)
     for da in range(1, near):
         hids.append(send(side_ref, side.at[lo], d_send.at[da], d_recv.at[da], across(da)))
         hids.append(send(hid_ref, hid.at[da - 1], h_send.at[da], h_recv.at[da], across(da)))
+    push(1)
 
     side[lo] = side_ref[...]
     top, low = split(hid_ref[...])
@@ -82,8 +88,8 @@
 
     relays = {}
 
-    def relay(dh):
-        for dg in range(peers):
+    def relay(dh, first_dg, last_dg):
+        for dg in range(first_dg, last_dg):
             source = lax.rem(me + peers - dg, peers)
             if (dh, dg) == (0, 0):
                 own_copy.wait()
@@ -129,7 +135,7 @@
         for dg in range(peers):
             relays[dh, dg].wait_recv()
 
-    relay(0)
+    relay(0, 0, peers)
     for copy in hids:
         copy.wait_recv()
     for da in range(1, near):
@@ -138,9 +144,10 @@
         h_hi[mid] = top
         h_lo[mid] = low
     forward(0, 0)
+    relay(1, 0, peers // 2)
     wait_relays(0)
-    relay(1)
     forward(0, 1)
+    relay(1, peers // 2, peers)
     forward(1, 0)
     wait_relays(1)
     forward(1, 1)

time: 98.6 us -> 101 us (1.024); the launches traced: 97 us -> 101 us
  Pallas kernels: 81.4 us -> 85.2 us
    pallas_call x1, Pallas kernels: 81.4 us -> 85.2 us  [local(): pl.pallas_call(functools.partial(kernel, peers, near, scale, piece), out_...]
where the time goes in v3:
time: 101 us
  Pallas kernels  85.2 us (84%)
  other arithmetic  7.58 us (8%)
  local copies, waits for them, and re-layouts  7.37 us (7%)
    pallas_call x1, Pallas kernels, local(): pl.pallas_call(functools.partial(kernel, peers, near, scale, piece), out_...  85.2 us
    scatter-add x1, other arithmetic, local(): grad_table = jnp.zeros(table.shape, f32).at[flat_ids].add(returned.reshap...  6.21 us
    gather x1, local copies, waits for them, and re-layouts, local(): table.at[flat_ids].get(mode='promise_in_bounds').reshape(peers, per, width)  4.41 us

profile of v3, /device:TPU:0, one launch (start us, length us, event | category | flops | bytes accessed | tf_op | source)
XLA Modules:
  0.0 100.8 jit_solution(14435380125592295711)
XLA Ops:
  0.6 0.7 compare_select_fusion
  1.3 0.0 copy-start.1
  1.3 0.7 convert_element_type.3
  2.0 0.0 copy-done.1
  2.0 1.6 %stack.8.side_ref = f32[8,512]{1,0:T(8,128)} concatenate(f32[1,512]{1,0:T(1,128)S(1)} %bitcast.17, f32[1,512]{1,0:T(1,128)} %bitcast.8, f32[1,512]{1,0:T(1,128)} %bitcast.9, f32[1,512]{1,0:T(1,128)} %bitcast.10, f32[1,512]{1,0:T(1,128)} %bitcast.11, f32[1,512]{1,0:T(1,128)} %bitcast.12, f32[1,512]{1,0:T(1,128)} %bitcast.13, f32[1,512]{1,0:T(1,128)} %bitcast.14), dimensions={0} | concatenate | bytes 32768 | tf_op jit(solution)/shard_map/stack | solution.py:281
  3.6 4.4 %gather_fusion = f32[512,256]{1,0:T(8,128)} fusion(f32[4096,256]{1,0:T(8,128)} %param.5, s32[1024]{0:T(1024)S(1)} %pad_clamp_fusion), kind=kCustom, calls=%fused_computation | custom fusion | bytes 1050624 | tf_op jit(solution)/shard_map/gather | solution.py:280
  8.0 85.2 %shard_map.76 = (f32[1,512]{1,0:T(1,128)}, f32[512,256]{1,0:T(8,128)}, f32[4,128,256]{2,1,0:T(8,128)}) custom-call(f32[4,128,256]{2,1,0:T(8,128)} %bitcast.7, f32[512,256]{1,0:T(8,128)} %hid_ref.1, f32[8,512]{1,0:T(8,128)} %stack.8.side_ref), custom_call_target="tpu_custom_call" | custom-call | flops 9663676416 | bytes 524288 | tf_op jit(solution)/shard_map/pallas_call | solution.py:287
  93.2 0.0 copy-start.2
  93.2 0.0 copy-start
  93.2 6.2 %scatter_custom_fusion = f32[4096,256]{1,0:T(8,128)} fusion(s32[512]{0:T(512)} %bitcast.16, f32[512,256]{1,0:T(8,128)} %bitcast.20, f32[]{:T(128)} %constant.2.clone.1), kind=kCustom, calls=%fused_computation.2 | custom fusion | flops 131072 | bytes 4194816 | tf_op jit(solution)/shard_map/scatter-add | solution.py:324
  99.5 0.0 copy-done.2
  99.5 0.6 copy.10
  100.0 0.0 copy-done
  100.0 0.8 copy.11
  (1 shorter events, 0.0 us)
Async XLA Ops:
  1.3 0.7 copy-start.1
  93.2 6.2 %copy-start.2 = (f32[1,512]{1,0:T(1,128)S(1)}, f32[1,512]{1,0:T(1,128)}, u32[]{:S(2)}) copy-start(f32[1,512]{1,0:T(1,128)} %get-tuple-element.6) | copy-start | bytes 6148
  93.2 6.8 %copy-start = (f32[512,256]{1,0:T(8,128)S(1)}, f32[512,256]{1,0:T(8,128)}, u32[]{:S(2)}) copy-start(f32[512,256]{1,0:T(8,128)} %get-tuple-element.13) | copy-start | bytes 1572868
